TPU v7x, 128 devices: a whole 4x4x4 slice. The times are simulated.
128 devices in a mesh: atom: 8 (over x, core), aux: 16 (over z, y).
Axes of the slice: x: 4, y: 4, z: 4, core: 2. Of those that a mesh axis runs over, the one named last changes fastest.
Arguments:
- three_index: bfloat16 [256, 16, 4, 128, 128], P('aux', 'atom'), may hold values from -0.09375 to 0.09375
- density: bfloat16 [2048, 2048], P(('atom', 'aux')), may hold values from -6 to 6
- pair_blocks: int32 [16, 4], replicated, may hold values from 0 to 15, as said below
- basis_counts: int32 [16], replicated, may hold values from 1 to 128, 1536 in all
Outputs:
- exchange_matrix: float32 [2048, 2048], P(('atom', 'aux'))
Inputs may be any that keep to these rules, and one draw needn't show every extreme that they name: `pair_blocks`: each row names 4 different basis blocks, the first being the row's own block.
All inputs are finite; a program needn't handle non-finite values.
Results may differ from a plain program's by a relative error of at most 0.0029.
Values may be sent and summed in bfloat16 or wider, within the bound.
No kernel may reach another device: no remote copies, remote signals or barrier semaphores. Data moves between devices by JAX's collectives and lax.ppermute only.
A program may use at most 192 MiB of HBM per device.

v0:
```python
import math
import jax
import jax.numpy as jnp
from jax import lax
from jax.sharding import PartitionSpec as P


def split_up(value, dim, size):
    lengths = value.shape
    parts = value.reshape(*lengths[:dim], size, lengths[dim] // size, *lengths[dim + 1 :])
    return jnp.moveaxis(parts, dim, 0)


def sent_and_summed(value, axis, dim):
    size = lax.axis_size(axis)
    parts = lax.all_to_all(split_up(value, dim, size), axis, 0, 0, tiled=True)
    return jnp.sum(parts, axis=0)


def per_device(three_index, density, pair_blocks, basis_counts):
    whole_density = lax.all_gather(density, ("atom", "aux"), axis=0, tiled=True)
    block_size = three_index.shape[-1]
    total_basis = whole_density.shape[1]
    total_blocks = total_basis // block_size
    own_blocks = three_index.shape[1]
    aux_here = three_index.shape[0]
    first_block = lax.axis_index("atom") * own_blocks
    live_slots = (jnp.arange(block_size)[None, :] < basis_counts[:, None]).astype(jnp.bfloat16)

    def masked(portion, offset):
        block_count = portion.shape[1]
        row_live = lax.dynamic_slice_in_dim(live_slots, offset, block_count, 0)
        partners = lax.dynamic_slice_in_dim(pair_blocks, offset, block_count, 0)
        col_live = live_slots[partners]
        cleaned = portion * row_live[None, :, None, :, None] * col_live[None, :, :, None, :]
        return (cleaned, partners)

    own_tensor, own_partners = masked(three_index, first_block)
    near_density = whole_density.reshape(total_blocks, block_size, total_basis)[own_partners]
    group_size = math.gcd(aux_here, 8)
    grouped = own_tensor.reshape((aux_here // group_size, group_size) + own_tensor.shape[1:])

    def contract(portion):
        product = jnp.einsum(
            "pmjab,mjbs->pmas", portion, near_density, preferred_element_type=jnp.float32
        )
        return product.astype(jnp.bfloat16)

    halfway = lax.map(contract, grouped).reshape(aux_here, own_blocks * block_size, total_basis)
    halfway_cols = halfway.reshape(aux_here, own_blocks * block_size, total_blocks, block_size)
    portion = lax.all_gather(three_index, "atom", axis=1, tiled=True)
    block_count = portion.shape[1]
    cleaned, partners = masked(portion, jnp.int32(0))
    contrib = jnp.einsum(
        "pmbc,pbjcn->mbjn", halfway_cols, cleaned, preferred_element_type=jnp.float32
    )
    placement = (partners.reshape(-1)[:, None] == jnp.arange(total_blocks)[None, :]).astype(
        jnp.float32
    )
    spread_out = jnp.einsum(
        "mqn,qk->mkn",
        contrib.reshape(contrib.shape[0], -1, block_size),
        placement,
        precision=lax.Precision.HIGHEST,
    )
    row_sums = spread_out.reshape(contrib.shape[0], total_basis)
    return sent_and_summed(row_sums, "aux", 0)


def solution(mesh):
    in_specs = (P("aux", "atom", None, None, None), P(("atom", "aux"), None), P(), P())
    out_specs = P(("atom", "aux"), None)
    return jax.shard_map(
        per_device, mesh=mesh, in_specs=in_specs, out_specs=out_specs, check_vma=False
    )
```

profile of v0, /device:TPU:0, one launch (start us, length us, event | category | flops | bytes accessed | tf_op | source)
XLA Modules:
  0.0 328.8 jit_solution(8203879094852832548)
XLA Ops:
  6.5 0.0 all-gather.5.cloned.1.call-start
  6.5 0.7 all-gather.5.cloned.1.call-update
  7.3 0.0 all-gather.3.cloned.1.call-start
  7.3 0.7 all-gather.3.cloned.1.call-update
  8.0 0.8 copy.10
  8.8 0.8 compare_select_fusion
  9.5 0.1 copy.12
  9.6 0.1 reshape.48
  9.7 0.7 compare_select_fusion.1
  10.4 0.1 copy.11
  10.5 0.1 reshape.40
  10.6 0.7 fusion.7
  11.3 0.6 gather_fusion.1
  11.9 0.6 gather_fusion
  12.5 0.1 eq.15
  12.6 4.5 %multiply_multiply_fusion.1 = bf16[16,2,4,128,128]{4,3,2,1,0:T(8,128)(2,1)} fusion(bf16[16,2,4,128,128]{4,3,2,1,0:T(8,128)(2,1)} %param.6, bf16[2,4,128]{2,1,0:T(4,128)(2,1)S(1)} %bitcast.57, bf16[2,128]{1,0:T(2,128)(2,1)S(1)} %constant_dynamic-slice_fusion.1), kind=kLoop, calls=%fused_computation.14 | loop fusion | flops 4194304 | bytes 8391168 | tf_op jit(solution)/shard_map/mul | solution.py:35
  17.2 66.0 %all-gather.5.cloned.1.call-done = bf16[2048,2048]{1,0:T(8,128)(2,1)} async-done(((bf16[16,2048]{1,0:T(8,128)(2,1)}), bf16[2048,2048]{1,0:T(8,128)(2,1)}) %all-gather.5.cloned.1.call-update) | async-done | bytes 8388624 | tf_op jit(solution)/shard_map/all_gather | solution.py:21
  83.2 6.1 %gather_fusion.2 = bf16[8,128,2048]{2,1,0:T(8,128)(2,1)} fusion(bf16[16,128,2048]{2,1,0:T(8,128)(2,1)} %bitcast.55, s32[1024]{0:T(1024)S(1)} %pad_clamp_fusion), kind=kCustom, calls=%fused_computation.2 | custom fusion | bytes 8388640 | tf_op jit(solution)/shard_map/gather | solution.py:39
  89.3 37.6 %while.10 = (s32[]{:T(128)}, bf16[2,8,2,128,2048]{4,3,2,1,0:T(8,128)(2,1)}, bf16[2,8,2,4,128,128]{5,4,3,2,1,0:T(8,128)(2,1)}, bf16[2,4,128,2048]{3,2,1,0:T(8,128)(2,1)}, s32[]{:T(128)}) while((s32[]{:T(128)}, bf16[2,8,2,128,2048]{4,3,2,1,0:T(8,128)(2,1)}, bf16[2,8,2,4,128,128]{5,4,3,2,1,0:T(8,128)(2,1)}, bf16[2,4,128,2048]{3,2,1,0:T(8,128)(2,1)}, ...), condition=%wide.region_1.2_spmd, body=%wide.region_0.1_spmd.sunk | while | flops 4299161600 | bytes 31458364 | solution.py:49
  89.3 9.7 %fusion.13 = bf16[1,8,2,128,2048]{4,3,1,2,0:T(8,128)(2,1)} fusion(bf16[2,4,128,2048]{3,2,1,0:T(8,128)(2,1)} %get-tuple-element.78, bf16[2,8,2,4,128,128]{5,4,3,2,1,0:T(8,128)(2,1)} %get-tuple-element.77, s32[]{:T(128)} %get-tuple-element.70), kind=kOutput, calls=%fused_computation.4.clone.1 | convolution fusion | flops 4299161600 | bytes 14680576 | tf_op jit(solution)/shard_map/while/body/eval_jaxpr/pmjab,mjbs->pmas/dot_general | solution.py:44
  99.0 10.4 %copy_dynamic-update-slice_fusion.2 = bf16[2,8,2,128,2048]{4,3,2,1,0:T(8,128)(2,1)} fusion(bf16[2,8,2,128,2048]{4,3,2,1,0:T(8,128)(2,1)} %get-tuple-element.71, s32[]{:T(128)} %get-tuple-element.70, bf16[1,8,2,128,2048]{4,3,1,2,0:T(8,128)(2,1)} %fusion.13), kind=kLoop, calls=%fused_computation.5.clone.1 | loop fusion | bytes 16777728 | tf_op jit(solution)/shard_map/while/body/jit(dynamic_update_index_in_dim)/dynamic_update_slice | solution.py:49
  109.4 9.2 %fusion.13 = bf16[1,8,2,128,2048]{4,3,1,2,0:T(8,128)(2,1)} fusion(bf16[2,4,128,2048]{3,2,1,0:T(8,128)(2,1)} %get-tuple-element.78, bf16[2,8,2,4,128,128]{5,4,3,2,1,0:T(8,128)(2,1)} %get-tuple-element.77, s32[]{:T(128)} %get-tuple-element.70), kind=kOutput, calls=%fused_computation.4.clone.1 | convolution fusion | flops 4299161600 | bytes 14680576 | tf_op jit(solution)/shard_map/while/body/eval_jaxpr/pmjab,mjbs->pmas/dot_general | solution.py:44
  118.7 8.2 %copy_dynamic-update-slice_fusion.2 = bf16[2,8,2,128,2048]{4,3,2,1,0:T(8,128)(2,1)} fusion(bf16[2,8,2,128,2048]{4,3,2,1,0:T(8,128)(2,1)} %get-tuple-element.71, s32[]{:T(128)} %get-tuple-element.70, bf16[1,8,2,128,2048]{4,3,1,2,0:T(8,128)(2,1)} %fusion.13), kind=kLoop, calls=%fused_computation.5.clone.1 | loop fusion | bytes 16777728 | tf_op jit(solution)/shard_map/while/body/jit(dynamic_update_index_in_dim)/dynamic_update_slice | solution.py:49
  126.9 9.9 %copy.29 = bf16[512,8,16,128]{3,2,1,0:T(8,128)(2,1)S(1)} copy(bf16[512,8,16,128]{3,1,2,0:T(8,128)(2,1)} %bitcast.52) | data formatting | bytes 33554432
  136.8 7.4 %bitcast_bitcast_fusion = bf16[16,256,16,128,1]{3,2,1,0,4:T(8,128)(2,1)} fusion(bf16[16,256,16,128]{3,2,1,0:T(8,128)(2,1)S(1)} %bitcast.50), kind=kLoop, calls=%fused_computation.12 | loop fusion | bytes 33554432 | tf_op jit(solution)/shard_map/reshape;reshape | solution.py:50
  144.3 94.0 %all-gather.3.cloned.1.call-done = bf16[16,16,4,128,128]{4,3,2,1,0:T(8,128)(2,1)} async-done(((bf16[16,2,4,128,128]{4,3,2,1,0:T(8,128)(2,1)}), bf16[16,16,4,128,128]{4,3,2,1,0:T(8,128)(2,1)}) %all-gather.3.cloned.1.call-update) | async-done | bytes 33554448 | tf_op jit(solution)/shard_map/all_gather | solution.py:51
  238.2 24.2 %fusion.2 = f32[16,4,128,256,1]{3,2,0,1,4:T(8,128)} fusion(bf16[16,256,16,128,1]{3,2,1,0,4:T(8,128)(2,1)} %bitcast_bitcast_fusion, bf16[16,16,4,128,128]{4,3,2,1,0:T(8,128)(2,1)} %all-gather.3.cloned.1.call-done, bf16[16,4,128]{2,1,0:T(4,128)(2,1)S(1)} %bitcast.56, bf16[16,128]{1,0:T(8,128)(2,1)S(1)} %fusion.7), kind=kOutput, calls=%fused_computation.9 | convolution fusion | flops 8623489024 | bytes 58740736 | tf_op jit(solution)/shard_map/pmbc,pbjcn->mbjn/dot_general | solution.py:54
  262.4 7.6 %copy.22 = f32[16,4,128,256,1]{3,2,1,0,4:T(8,128)} copy(f32[16,4,128,256,1]{3,2,0,1,4:T(8,128)} %fusion.2) | data formatting | bytes 16777216 | tf_op jit(solution)/shard_map/pmbc,pbjcn->mbjn/dot_general | solution.py:54
  270.0 8.7 %copy.17 = f32[256,64,128]{2,1,0:T(8,128)} copy(f32[256,64,128]{0,2,1:T(8,128)} %bitcast.51) | data formatting | bytes 16777216 | tf_op jit(solution)/shard_map/reshape | solution.py:62
  278.8 5.1 %convolution_bitcast_fusion = f32[256,16,128]{2,1,0:T(8,128)S(1)} fusion(f32[256,64,128]{2,1,0:T(8,128)} %copy.17, s32[64]{0:T(128)S(1)} %eq.15), kind=kOutput, calls=%fused_computation.15 | convolution fusion | flops 402654208 | bytes 10486016 | tf_op jit(solution)/shard_map/mqn,qk->mkn/dot_general | solution.py:60
  283.9 1.5 reshape_reshape.7
  285.4 35.8 %all_to_all.5 = f32[16,16,2048]{2,1,0:T(8,128)S(1)} all-to-all(f32[16,16,2048]{2,1,0:T(8,128)} %reshape_reshape.7), channel_id=1, replica_groups=mesh['atom'=8,'aux'=16] {'aux'}, dimensions={0} | all-to-all | bytes 4194304 | tf_op jit(solution)/shard_map/all_to_all | solution.py:16
  321.2 0.8 reduce_sum.9
  (4 shorter events, 0.0 us)
Async XLA Ops:
  6.5 76.6 %all-gather.5.cloned.1.call-start = ((), (), s32[]{:S(2)}) async-start(), calls=%async_computation.2 | async-start | bytes 8454144 | tf_op jit(solution)/shard_map/all_gather | solution.py:21
  7.3 231.0 %all-gather.3.cloned.1.call-start = ((), (), s32[]{:S(2)}) async-start(), calls=%async_computation.1 | async-start | bytes 37748736 | tf_op jit(solution)/shard_map/all_gather | solution.py:51
Sparse Core Ops, SparseCore 0:
  10.5 72.6 all-gather.4
  84.8 153.3 all-gather.2
where the time goes:
time: 329 us
  waiting for transfers between devices  161 us (49%)
  local copies, waits for them, and re-layouts  62.4 us (19%)
  matrix products  48.3 us (15%)
  blocking collectives  35.8 us (11%)
  between operations  13.5 us (4%)
  other arithmetic  7.45 us (2%)
    all_gather x1, waiting for transfers between devices, per_device(): portion = lax.all_gather(three_index, 'atom', axis=1, tiled=True)  94 us
    all_gather x1, waiting for transfers between devices, per_device(): whole_density = lax.all_gather(density, ('atom', 'aux'), axis=0, tiled=True)  66 us
    all_to_all x1, blocking collectives, sent_and_summed(): parts = lax.all_to_all(split_up(value, dim, size), axis, 0, 0, tiled=True)  35.8 us
    dot_general x1, matrix products, per_device(): jnp.einsum('pmbc,pbjcn->mbjn', halfway_cols, cleaned, preferred_element_t...  24.2 us
    dot_general x2, matrix products, contract(): jnp.einsum('pmjab,mjbs->pmas', portion, near_density, preferred_element_t...  18.9 us
    dynamic_update_slice x2, local copies, waits for them, and re-layouts, per_device(): lax.map(contract, grouped)  18.7 us
    unnamed x2, local copies, waits for them, and re-layouts  10.7 us
    reshape x1, local copies, waits for them, and re-layouts, per_device(): contrib.reshape(contrib.shape[0], -1, block_size)  8.72 us
  transfers between devices with their start and end apart: 2, of which 2 were waited for; matrix products, arithmetic and copies ran while one was open for 21% of the time, Pallas kernels for 0%

commit v1 on v0

--- a/solution.py
+++ b/solution.py
@@ -48,7 +48,16 @@
 
     halfway = lax.map(contract, grouped).reshape(aux_here, own_blocks * block_size, total_basis)
     halfway_cols = halfway.reshape(aux_here, own_blocks * block_size, total_blocks, block_size)
-    portion = lax.all_gather(three_index, "atom", axis=1, tiled=True)
+    ways = lax.axis_size("atom")
+    up = [(d, (d + 1) % ways) for d in range(ways)]
+    down = [(d, (d - 1) % ways) for d in range(ways)]
+    earlier, later = ([three_index], [three_index])
+    for _ in range(ways // 2):
+        earlier.append(lax.ppermute(earlier[-1], "atom", up))
+    for _ in range((ways - 1) // 2):
+        later.append(lax.ppermute(later[-1], "atom", down))
+    line = jnp.concatenate([*earlier[::-1], *later[1:]], axis=1)
+    portion = jnp.roll(line, (lax.axis_index("atom") - ways // 2) * three_index.shape[1], axis=1)
     block_count = portion.shape[1]
     cleaned, partners = masked(portion, jnp.int32(0))
     contrib = jnp.einsum(

time: 329 us -> 436 us (1.33)
  local copies, waits for them, and re-layouts: 62.4 us -> 134 us
  waiting for transfers between devices: 161 us -> 189 us
  starting transfers between devices: 0.04 us -> 9.11 us
  blocking collectives: 35.8 us -> 31.1 us
    ppermute x0 -> x7, waiting for transfers between devices: none -> 189 us  [the longest x4 187 us: per_device(): earlier.append(lax.ppermute(earlier[-1], 'atom', up))]
    all_gather x1 -> x0, waiting for transfers between devices: 94 us -> none  [per_device(): portion = lax.all_gather(three_index, 'atom', axis=1, tiled=True)]
    unnamed x2 -> x30, local copies, waits for them, and re-layouts: 10.7 us -> 77.7 us
    all_gather x1, waiting for transfers between devices: 66 us -> 0.01 us  [per_device(): whole_density = lax.all_gather(density, ('atom', 'aux'), axis=0, tiled=True)]
    ppermute x0 -> x7, starting transfers between devices: none -> 9.11 us  [the longest x3 9.1 us: per_device(): later.append(lax.ppermute(later[-1], 'atom', down))]
    concatenate x0 -> x1, local copies, waits for them, and re-layouts: none -> 5.74 us  [per_device(): jnp.roll(line, (lax.axis_index('atom') - ways // 2) * three_index.shape[1...]
    all_to_all x1, blocking collectives: 35.8 us -> 31.1 us  [sent_and_summed(): parts = lax.all_to_all(split_up(value, dim, size), axis, 0, 0, tiled=True)]
  transfers between devices with their start and end apart: 2 -> 8, of which waited for: 2 -> 5; matrix products, arithmetic and copies ran while one was open for 21% -> 10% of each run, Pallas kernels for 0% -> 0%
where the time goes in v1:
time: 436 us; the launch traced here: 433 us
  waiting for transfers between devices  189 us (43%)
  local copies, waits for them, and re-layouts  134 us (31%)
  matrix products  47.9 us (11%)
  blocking collectives  31.1 us (7%)
  between operations  13.5 us (3%)
  starting transfers between devices  9.11 us (2%)
  other arithmetic  8.08 us (2%)
    ppermute x4, waiting for transfers between devices, per_device(): earlier.append(lax.ppermute(earlier[-1], 'atom', up))  187 us
    unnamed x30, local copies, waits for them, and re-layouts  77.7 us
    all_to_all x1, blocking collectives, sent_and_summed(): parts = lax.all_to_all(split_up(value, dim, size), axis, 0, 0, tiled=True)  31.1 us
    dot_general x1, matrix products, per_device(): jnp.einsum('pmbc,pbjcn->mbjn', halfway_cols, cleaned, preferred_element_t...  24.3 us
    dot_general x2, matrix products, contract(): jnp.einsum('pmjab,mjbs->pmas', portion, near_density, preferred_element_t...  18.5 us
    dynamic_update_slice x2, local copies, waits for them, and re-layouts, per_device(): lax.map(contract, grouped)  16.6 us
    ppermute x3, starting transfers between devices, per_device(): later.append(lax.ppermute(later[-1], 'atom', down))  9.1 us
  transfers between devices with their start and end apart: 8, of which 5 were waited for; matrix products, arithmetic and copies ran while one was open for 10% of the time, Pallas kernels for 0%

profile of v1, /device:TPU:0, one launch (start us, length us, event | category | flops | bytes accessed | tf_op | source)
XLA Modules:
  0.0 433.2 jit_solution(10814164402533080486)
XLA Ops:
  6.5 0.0 all-gather.2.cloned.1.call-start
  6.5 0.0 collective-permute-start
  6.5 0.7 all-gather.2.cloned.1.call-update
  7.3 52.2 %collective-permute-done = bf16[16,2,4,128,128]{4,3,2,1,0:T(8,128)(2,1)} collective-permute-done((bf16[16,2,4,128,128]{4,3,2,1,0:T(8,128)(2,1)}, bf16[16,2,4,128,128]{4,3,2,1,0:T(8,128)(2,1)}, u32[]{:S(2)}, u32[]{:S(2)}) %collective-permute-start) | collective-permute-done | bytes 4194336 | tf_op jit(solution)/shard_map/ppermute | solution.py:56
  59.5 0.0 collective-permute-start.1
  59.5 3.0 collective-permute-start.4
  62.4 57.5 %collective-permute-done.1 = bf16[16,2,4,128,128]{4,3,2,1,0:T(8,128)(2,1)S(1)} collective-permute-done((bf16[16,2,4,128,128]{4,3,2,1,0:T(8,128)(2,1)}, bf16[16,2,4,128,128]{4,3,2,1,0:T(8,128)(2,1)S(1)}, u32[]{:S(2)}, u32[]{:S(2)}) %collective-permute-start.1) | collective-permute-done | bytes 4194336 | tf_op jit(solution)/shard_map/ppermute | solution.py:56
  119.9 0.0 collective-permute-start.2
  119.9 0.0 collective-permute-done.4
  119.9 0.0 copy-start
  119.9 2.0 copy-done
  121.9 2.9 collective-permute-start.5
  124.8 44.3 %collective-permute-done.2 = bf16[16,2,4,128,128]{4,3,2,1,0:T(8,128)(2,1)} collective-permute-done((bf16[16,2,4,128,128]{4,3,2,1,0:T(8,128)(2,1)S(1)}, bf16[16,2,4,128,128]{4,3,2,1,0:T(8,128)(2,1)}, u32[]{:S(2)}, u32[]{:S(2)}) %collective-permute-start.2) | collective-permute-done | bytes 4194336 | tf_op jit(solution)/shard_map/ppermute | solution.py:56
  169.1 0.0 collective-permute-start.3
  169.1 1.7 collective-permute-done.5
  170.8 0.0 copy-done.3
  170.8 3.2 collective-permute-start.6
  174.1 0.8 copy.10
  174.8 0.8 compare_select_fusion
  175.6 0.1 copy.12
  175.7 0.1 reshape.48
  175.8 0.7 compare_select_fusion.1
  176.4 0.1 copy.11
  176.5 0.1 reshape.40
  176.6 0.7 fusion.7
  177.4 0.6 gather_fusion.1
  177.9 0.6 gather_fusion
  178.6 0.7 eq.18
  179.2 6.3 %gather_fusion.2 = bf16[8,128,2048]{2,1,0:T(8,128)(2,1)} fusion(bf16[16,128,2048]{2,1,0:T(8,128)(2,1)} %bitcast.55, s32[1024]{0:T(1024)S(1)} %pad_clamp_fusion), kind=kCustom, calls=%fused_computation.2 | custom fusion | bytes 8388640 | tf_op jit(solution)/shard_map/gather | solution.py:39
  185.5 33.1 %collective-permute-done.3 = bf16[16,2,4,128,128]{4,3,2,1,0:T(8,128)(2,1)} collective-permute-done((bf16[16,2,4,128,128]{4,3,2,1,0:T(8,128)(2,1)}, bf16[16,2,4,128,128]{4,3,2,1,0:T(8,128)(2,1)}, u32[]{:S(2)}, u32[]{:S(2)}) %collective-permute-start.3) | collective-permute-done | bytes 4194336 | tf_op jit(solution)/shard_map/ppermute | solution.py:56
  218.6 5.7 %constant_dynamic-update-slice_fusion.15 = bf16[16,32,4,128,128]{4,3,2,1,0:T(8,128)(2,1)} fusion(bf16[16,2,4,128,128]{4,3,2,1,0:T(8,128)(2,1)} %collective-permute-done.3), kind=kLoop, calls=%fused_computation.31 | loop fusion | bytes 8388608
  224.3 5.7 %constant_dynamic-update-slice_fusion.14 = bf16[16,32,4,128,128]{4,3,2,1,0:T(8,128)(2,1)} fusion(bf16[16,32,4,128,128]{4,3,2,1,0:T(8,128)(2,1)} %constant_dynamic-update-slice_fusion.15, bf16[16,2,4,128,128]{4,3,2,1,0:T(8,128)(2,1)} %collective-permute-done.2), kind=kLoop, calls=%fused_computation.30 | loop fusion | bytes 8388608
  229.9 0.0 copy-done.4
  229.9 2.8 constant_dynamic-update-slice_fusion.13
  232.7 5.7 %constant_dynamic-update-slice_fusion.12 = bf16[16,32,4,128,128]{4,3,2,1,0:T(8,128)(2,1)} fusion(bf16[16,32,4,128,128]{4,3,2,1,0:T(8,128)(2,1)} %constant_dynamic-update-slice_fusion.13, bf16[16,2,4,128,128]{4,3,2,1,0:T(8,128)(2,1)} %collective-permute-done), kind=kLoop, calls=%fused_computation.28 | loop fusion | bytes 8388608
  238.4 5.1 %multiply_multiply_fusion.1 = (bf16[16,2,4,128,128]{4,3,2,1,0:T(8,128)(2,1)}, bf16[16,32,4,128,128]{4,3,2,1,0:T(8,128)(2,1)}) fusion(bf16[16,2,4,128,128]{4,3,2,1,0:T(8,128)(2,1)S(1)} %copy-done.5, bf16[2,4,128]{2,1,0:T(4,128)(2,1)S(1)} %bitcast.57, bf16[2,128]{1,0:T(2,128)(2,1)S(1)} %constant_dynamic-slice_fusion.1, ...), kind=kLoop, calls=%fused_computation.14 | loop fusion | flops 12582912 | bytes 12585472 | tf_op jit(solution)/shard_map/mul | solution.py:35
  243.6 2.8 constant_dynamic-update-slice_fusion.10
  246.3 5.7 %constant_dynamic-update-slice_fusion.9 = bf16[16,32,4,128,128]{4,3,2,1,0:T(8,128)(2,1)} fusion(bf16[16,32,4,128,128]{4,3,2,1,0:T(8,128)(2,1)} %constant_dynamic-update-slice_fusion.10, bf16[16,2,4,128,128]{4,3,2,1,0:T(8,128)(2,1)} %collective-permute-done.5), kind=kLoop, calls=%fused_computation.25 | loop fusion | bytes 8388608
  252.1 0.0 collective-permute-done.6
  252.1 5.7 %constant_dynamic-update-slice_fusion.8 = bf16[16,32,4,128,128]{4,3,2,1,0:T(8,128)(2,1)} fusion(bf16[16,32,4,128,128]{4,3,2,1,0:T(8,128)(2,1)} %constant_dynamic-update-slice_fusion.9, bf16[16,2,4,128,128]{4,3,2,1,0:T(8,128)(2,1)} %collective-permute-done.6), kind=kLoop, calls=%fused_computation.24 | loop fusion | bytes 8388608
  257.8 5.7 %constant_dynamic-update-slice_fusion.7 = bf16[16,32,4,128,128]{4,3,2,1,0:T(8,128)(2,1)} fusion(bf16[16,32,4,128,128]{4,3,2,1,0:T(8,128)(2,1)} %constant_dynamic-update-slice_fusion.8, bf16[16,2,4,128,128]{4,3,2,1,0:T(8,128)(2,1)} %collective-permute-done.3), kind=kLoop, calls=%fused_computation.23 | loop fusion | bytes 8388608
  263.4 5.7 %constant_dynamic-update-slice_fusion.6 = bf16[16,32,4,128,128]{4,3,2,1,0:T(8,128)(2,1)} fusion(bf16[16,32,4,128,128]{4,3,2,1,0:T(8,128)(2,1)} %constant_dynamic-update-slice_fusion.7, bf16[16,2,4,128,128]{4,3,2,1,0:T(8,128)(2,1)} %collective-permute-done.2), kind=kLoop, calls=%fused_computation.22 | loop fusion | bytes 8388608
  269.2 2.7 constant_dynamic-update-slice_fusion.5
  271.9 5.8 %constant_dynamic-update-slice_fusion.4 = bf16[16,32,4,128,128]{4,3,2,1,0:T(8,128)(2,1)} fusion(bf16[16,32,4,128,128]{4,3,2,1,0:T(8,128)(2,1)} %constant_dynamic-update-slice_fusion.5, bf16[16,2,4,128,128]{4,3,2,1,0:T(8,128)(2,1)} %collective-permute-done), kind=kLoop, calls=%fused_computation.20 | loop fusion | bytes 8388608
  277.8 2.8 constant_dynamic-update-slice_fusion.3
  280.5 35.2 %while.10 = (s32[]{:T(128)}, bf16[2,8,2,128,2048]{4,3,2,1,0:T(8,128)(2,1)}, bf16[2,8,2,4,128,128]{5,4,3,2,1,0:T(8,128)(2,1)}, bf16[2,4,128,2048]{3,2,1,0:T(8,128)(2,1)}, s32[]{:T(128)}) while((s32[]{:T(128)}, bf16[2,8,2,128,2048]{4,3,2,1,0:T(8,128)(2,1)}, bf16[2,8,2,4,128,128]{5,4,3,2,1,0:T(8,128)(2,1)}, bf16[2,4,128,2048]{3,2,1,0:T(8,128)(2,1)}, ...), condition=%wide.region_1.2_spmd, body=%wide.region_0.1_spmd.sunk | while | flops 4299161600 | bytes 31458364 | solution.py:49
  280.5 9.3 %fusion.13 = bf16[1,8,2,128,2048]{4,3,1,2,0:T(8,128)(2,1)} fusion(bf16[2,4,128,2048]{3,2,1,0:T(8,128)(2,1)} %get-tuple-element.80, bf16[2,8,2,4,128,128]{5,4,3,2,1,0:T(8,128)(2,1)} %get-tuple-element.79, s32[]{:T(128)} %get-tuple-element.72), kind=kOutput, calls=%fused_computation.4.clone.1 | convolution fusion | flops 4299161600 | bytes 14680576 | tf_op jit(solution)/shard_map/while/body/eval_jaxpr/pmjab,mjbs->pmas/dot_general | solution.py:44
  289.8 8.3 %copy_dynamic-update-slice_fusion.2 = bf16[2,8,2,128,2048]{4,3,2,1,0:T(8,128)(2,1)} fusion(bf16[2,8,2,128,2048]{4,3,2,1,0:T(8,128)(2,1)} %get-tuple-element.73, s32[]{:T(128)} %get-tuple-element.72, bf16[1,8,2,128,2048]{4,3,1,2,0:T(8,128)(2,1)} %fusion.13), kind=kLoop, calls=%fused_computation.5.clone.1 | loop fusion | bytes 16777728 | tf_op jit(solution)/shard_map/while/body/jit(dynamic_update_index_in_dim)/dynamic_update_slice | solution.py:49
  298.0 9.3 %fusion.13 = bf16[1,8,2,128,2048]{4,3,1,2,0:T(8,128)(2,1)} fusion(bf16[2,4,128,2048]{3,2,1,0:T(8,128)(2,1)} %get-tuple-element.80, bf16[2,8,2,4,128,128]{5,4,3,2,1,0:T(8,128)(2,1)} %get-tuple-element.79, s32[]{:T(128)} %get-tuple-element.72), kind=kOutput, calls=%fused_computation.4.clone.1 | convolution fusion | flops 4299161600 | bytes 14680576 | tf_op jit(solution)/shard_map/while/body/eval_jaxpr/pmjab,mjbs->pmas/dot_general | solution.py:44
  307.3 8.4 %copy_dynamic-update-slice_fusion.2 = bf16[2,8,2,128,2048]{4,3,2,1,0:T(8,128)(2,1)} fusion(bf16[2,8,2,128,2048]{4,3,2,1,0:T(8,128)(2,1)} %get-tuple-element.73, s32[]{:T(128)} %get-tuple-element.72, bf16[1,8,2,128,2048]{4,3,1,2,0:T(8,128)(2,1)} %fusion.13), kind=kLoop, calls=%fused_computation.5.clone.1 | loop fusion | bytes 16777728 | tf_op jit(solution)/shard_map/while/body/jit(dynamic_update_index_in_dim)/dynamic_update_slice | solution.py:49
  315.7 9.6 %copy.29 = bf16[512,8,16,128]{3,2,1,0:T(8,128)(2,1)S(1)} copy(bf16[512,8,16,128]{3,1,2,0:T(8,128)(2,1)} %bitcast.52) | data formatting | bytes 33554432
  325.3 0.0 copy-start.2
  325.3 7.6 %bitcast_bitcast_fusion = bf16[16,256,16,128,1]{3,2,1,0,4:T(8,128)(2,1)} fusion(bf16[16,256,16,128]{3,2,1,0:T(8,128)(2,1)S(1)} %bitcast.50), kind=kLoop, calls=%fused_computation.12 | loop fusion | bytes 33554432 | tf_op jit(solution)/shard_map/reshape;reshape | solution.py:50
  332.9 2.8 constant_dynamic-update-slice_fusion.2
  335.7 5.8 %constant_dynamic-update-slice_fusion.1 = bf16[16,32,4,128,128]{4,3,2,1,0:T(8,128)(2,1)} fusion(bf16[16,32,4,128,128]{4,3,2,1,0:T(8,128)(2,1)} %constant_dynamic-update-slice_fusion.2, bf16[16,2,4,128,128]{4,3,2,1,0:T(8,128)(2,1)} %collective-permute-done.5), kind=kLoop, calls=%fused_computation.17 | loop fusion | bytes 8388608
  341.5 5.7 %constant_dynamic-update-slice_fusion = bf16[16,32,4,128,128]{4,3,2,1,0:T(8,128)(2,1)} fusion(bf16[16,32,4,128,128]{4,3,2,1,0:T(8,128)(2,1)} %constant_dynamic-update-slice_fusion.1, bf16[16,2,4,128,128]{4,3,2,1,0:T(8,128)(2,1)} %collective-permute-done.6), kind=kLoop, calls=%fused_computation.16 | loop fusion | bytes 8388608 | tf_op jit(solution)/shard_map/jit(_roll_dynamic)/concatenate | solution.py:60
  347.2 24.3 %fusion.2 = f32[16,4,128,256,1]{3,2,0,1,4:T(8,128)} fusion(bf16[16,256,16,128,1]{3,2,1,0,4:T(8,128)(2,1)} %bitcast_bitcast_fusion, bf16[16,32,4,128,128]{4,3,2,1,0:T(8,128)(2,1)} %constant_dynamic-update-slice_fusion, s32[]{:T(128)S(6)} %select_n.25, bf16[16,4,128]{2,1,0:T(4,128)(2,1)S(1)} %bitcast.56, bf16[16,128]{1,0:T(8,128)(2,1)S(1)} %fusion.7), kind=kOutput, calls=%fused_computation.9 | convolution fusion | flops 8623489024 | bytes 58740740 | tf_op jit(solution)/shard_map/pmbc,pbjcn->mbjn/dot_general | solution.py:63
  371.5 7.6 %copy.22 = f32[16,4,128,256,1]{3,2,1,0,4:T(8,128)} copy(f32[16,4,128,256,1]{3,2,0,1,4:T(8,128)} %fusion.2) | data formatting | bytes 16777216 | tf_op jit(solution)/shard_map/pmbc,pbjcn->mbjn/dot_general | solution.py:63
  379.1 8.7 %copy.17 = f32[256,64,128]{2,1,0:T(8,128)} copy(f32[256,64,128]{0,2,1:T(8,128)} %bitcast.51) | data formatting | bytes 16777216 | tf_op jit(solution)/shard_map/reshape | solution.py:71
  387.8 0.0 copy-done.6
  387.9 5.1 %convolution_bitcast_fusion = f32[256,16,128]{2,1,0:T(8,128)S(1)} fusion(f32[256,64,128]{2,1,0:T(8,128)} %copy.17, s32[64]{0:T(128)S(1)} %copy-done.6), kind=kOutput, calls=%fused_computation.15 | convolution fusion | flops 402654208 | bytes 10486016 | tf_op jit(solution)/shard_map/mqn,qk->mkn/dot_general | solution.py:69
  393.0 1.5 reshape_reshape.7
  394.5 31.1 %all_to_all.5 = f32[16,16,2048]{2,1,0:T(8,128)S(1)} all-to-all(f32[16,16,2048]{2,1,0:T(8,128)} %reshape_reshape.7), channel_id=1, replica_groups=mesh['atom'=8,'aux'=16] {'aux'}, dimensions={0} | all-to-all | bytes 4194304 | tf_op jit(solution)/shard_map/all_to_all | solution.py:16
  425.6 0.8 reduce_sum.9
  (13 shorter events, 0.0 us)
Async XLA Ops:
  6.5 172.7 %all-gather.2.cloned.1.call-start = ((), (), s32[]{:S(2)}) async-start(), calls=%async_computation.1 | async-start | bytes 8454144 | tf_op jit(solution)/shard_map/all_gather | solution.py:21
  6.5 52.9 %collective-permute-start = (bf16[16,2,4,128,128]{4,3,2,1,0:T(8,128)(2,1)}, bf16[16,2,4,128,128]{4,3,2,1,0:T(8,128)(2,1)}, u32[]{:S(2)}, u32[]{:S(2)}) collective-permute-start(bf16[16,2,4,128,128]{4,3,2,1,0:T(8,128)(2,1)} %param.6), channel_id=1, source_target_pairs={{0,16},{16,32},{32,48},{48,64},{64,80},{80,96},{96,112},{112,0},{1... | collective-permute-start | bytes 12582920 | tf_op jit(solution)/shard_map/ppermute | solution.py:56
  59.5 60.4 %collective-permute-start.1 = (bf16[16,2,4,128,128]{4,3,2,1,0:T(8,128)(2,1)}, bf16[16,2,4,128,128]{4,3,2,1,0:T(8,128)(2,1)S(1)}, u32[]{:S(2)}, u32[]{:S(2)}) collective-permute-start(bf16[16,2,4,128,128]{4,3,2,1,0:T(8,128)(2,1)} %collective-permute-done), channel_id=1, source_target_pairs={{0,16},{16,32},{32,48},{48,64},{64,80},{80,96},{96,112},{112,0},{1... | collective-permute-start | bytes 12582920 | tf_op jit(solution)/shard_map/ppermute | solution.py:56
  59.5 60.4 %collective-permute-start.4 = (bf16[16,2,4,128,128]{4,3,2,1,0:T(8,128)(2,1)}, bf16[16,2,4,128,128]{4,3,2,1,0:T(8,128)(2,1)S(1)}, u32[]{:S(2)}, u32[]{:S(2)}) collective-permute-start(bf16[16,2,4,128,128]{4,3,2,1,0:T(8,128)(2,1)} %param.6), channel_id=1, source_target_pairs={{0,112},{16,0},{32,16},{48,32},{64,48},{80,64},{96,80},{112,96},{1... | collective-permute-start | bytes 12582920 | tf_op jit(solution)/shard_map/ppermute | solution.py:58
  119.9 50.9 %copy-start.3 = (bf16[16,2,4,128,128]{4,3,2,1,0:T(8,128)(2,1)}, bf16[16,2,4,128,128]{4,3,2,1,0:T(8,128)(2,1)S(1)}, u32[]{:S(2)}) copy-start(bf16[16,2,4,128,128]{4,3,2,1,0:T(8,128)(2,1)S(1)} %collective-permute-done.1) | copy-start | bytes 12582916
  119.9 49.2 %collective-permute-start.2 = (bf16[16,2,4,128,128]{4,3,2,1,0:T(8,128)(2,1)S(1)}, bf16[16,2,4,128,128]{4,3,2,1,0:T(8,128)(2,1)}, u32[]{:S(2)}, u32[]{:S(2)}) collective-permute-start(bf16[16,2,4,128,128]{4,3,2,1,0:T(8,128)(2,1)S(1)} %collective-permute-done.1), channel_id=1, source_target_pairs={{0,16},{16,32},{32,48},{48,64},{64,80},{80,96},{96,112},{112,0},{1... | collective-permute-start | bytes 12582920 | tf_op jit(solution)/shard_map/ppermute | solution.py:56
  119.9 2.0 copy-start
  121.9 48.9 %collective-permute-start.5 = (bf16[16,2,4,128,128]{4,3,2,1,0:T(8,128)(2,1)S(1)}, bf16[16,2,4,128,128]{4,3,2,1,0:T(8,128)(2,1)}, u32[]{:S(2)}, u32[]{:S(2)}) collective-permute-start(bf16[16,2,4,128,128]{4,3,2,1,0:T(8,128)(2,1)S(1)} %collective-permute-done.4), channel_id=1, source_target_pairs={{0,112},{16,0},{32,16},{48,32},{64,48},{80,64},{96,80},{112,96},{1... | collective-permute-start | bytes 12582920 | tf_op jit(solution)/shard_map/ppermute | solution.py:58
  169.1 49.5 %collective-permute-start.3 = (bf16[16,2,4,128,128]{4,3,2,1,0:T(8,128)(2,1)}, bf16[16,2,4,128,128]{4,3,2,1,0:T(8,128)(2,1)}, u32[]{:S(2)}, u32[]{:S(2)}) collective-permute-start(bf16[16,2,4,128,128]{4,3,2,1,0:T(8,128)(2,1)} %collective-permute-done.2), channel_id=1, source_target_pairs={{0,16},{16,32},{32,48},{48,64},{64,80},{80,96},{96,112},{112,0},{1... | collective-permute-start | bytes 12582920 | tf_op jit(solution)/shard_map/ppermute | solution.py:56
  170.8 81.2 %collective-permute-start.6 = (bf16[16,2,4,128,128]{4,3,2,1,0:T(8,128)(2,1)}, bf16[16,2,4,128,128]{4,3,2,1,0:T(8,128)(2,1)}, u32[]{:S(2)}, u32[]{:S(2)}) collective-permute-start(bf16[16,2,4,128,128]{4,3,2,1,0:T(8,128)(2,1)} %collective-permute-done.5), channel_id=1, source_target_pairs={{0,112},{16,0},{32,16},{48,32},{64,48},{80,64},{96,80},{112,96},{1... | collective-permute-start | bytes 12582920 | tf_op jit(solution)/shard_map/ppermute | solution.py:58
  185.5 44.4 %copy-start.4 = (bf16[16,2,4,128,128]{4,3,2,1,0:T(8,128)(2,1)S(1)}, bf16[16,2,4,128,128]{4,3,2,1,0:T(8,128)(2,1)}, u32[]{:S(2)}) copy-start(bf16[16,2,4,128,128]{4,3,2,1,0:T(8,128)(2,1)} %copy-done.3) | copy-start | bytes 12582916
  185.5 52.9 %copy-start.5 = (bf16[16,2,4,128,128]{4,3,2,1,0:T(8,128)(2,1)S(1)}, bf16[16,2,4,128,128]{4,3,2,1,0:T(8,128)(2,1)}, u32[]{:S(2)}) copy-start(bf16[16,2,4,128,128]{4,3,2,1,0:T(8,128)(2,1)} %param.6) | copy-start | bytes 12582916
  229.9 13.6 %copy-start.1 = (bf16[16,2,4,128,128]{4,3,2,1,0:T(8,128)(2,1)S(1)}, bf16[16,2,4,128,128]{4,3,2,1,0:T(8,128)(2,1)}, u32[]{:S(2)}) copy-start(bf16[16,2,4,128,128]{4,3,2,1,0:T(8,128)(2,1)} %copy-done) | copy-start | bytes 12582916
  325.3 7.6 %copy-start.2 = (bf16[16,2,4,128,128]{4,3,2,1,0:T(8,128)(2,1)S(1)}, bf16[16,2,4,128,128]{4,3,2,1,0:T(8,128)(2,1)}, u32[]{:S(2)}) copy-start(bf16[16,2,4,128,128]{4,3,2,1,0:T(8,128)(2,1)} %copy-done) | copy-start | bytes 12582916
  371.5 16.3 %copy-start.6 = (s32[64]{0:T(128)S(1)}, s32[64]{0:T(128)}, u32[]{:S(2)}) copy-start(s32[64]{0:T(128)} %eq.18) | copy-start | bytes 772
Sparse Core Ops, SparseCore 0:
  10.5 74.9 all-gather.1
